TPU v7x, 128 devices: a whole 4x4x4 slice. The times are simulated.
128 devices in a mesh: lat: 8 (over z, core), lon: 16 (over y, x).
Axes of the slice: x: 4, y: 4, z: 4, core: 2. Of those that a mesh axis runs over, the one named last changes fastest.
Arguments:
- ice_state: float32 [5, 2048, 4096], P(None, 'lat', 'lon'), may hold values from -6 to 6
- ocean_forcing: float32 [4, 2048, 4096], P(None, 'lat', 'lon'), may hold values from -6 to 6
- ice_strength: float32 [2048, 4096], P('lat', 'lon'), may hold values from 0.5 to 4
- ice_mask: int32 [2048, 4096], P('lat', 'lon'), may hold values from 0 to 1, as said below
- yield_mask: int32 [6, 2048, 4096], P(None, 'lat', 'lon'), may hold values 0 or 1
- ice_route: int32 [8, 8], replicated, may hold values from 0 to 7, each once within a row
Outputs:
- ocean_flux: float32 [2, 2048, 4096], P(None, 'lat', 'lon')
- ice_blocks: float32 [64, 5, 32, 4096], P('lat', None, None, 'lon')
Inputs may be any that keep to these rules, and one draw needn't show every extreme that they name: `ice_route`: each row is a permutation of 0 .. 7. `ice_mask`: ice is set block by block of 32 latitude rows: every block of the first and of the last latitude band may hold ice, and one or more blocks of every other band; in all other blocks it is 0.
All inputs are finite; a program needn't handle non-finite values. No bound on the sum of `yield_mask` on one device may be relied on, other than what follows from the above.
Results may differ from a plain program's by a relative error of at most 0.00011.
Values sent between devices are 32-bit elements; how exact they have to be, the bound alone decides.
A program may use at most 128 MiB of HBM per device.

v0:
```python
import functools

import jax
import jax.numpy as jnp
from jax import lax
from jax.experimental import pallas as pl
from jax.experimental.pallas import tpu as pltpu
from jax.sharding import PartitionSpec as P

RELAX_RATE = 1.0
STEP_WEIGHT = 0.5
DRAG_COEF = 0.5
CORIOLIS = 0.3

KEEP = 1.0 / (1.0 + RELAX_RATE)
DAMP = 1.0 / (1.0 + STEP_WEIGHT * DRAG_COEF)

MESH = pl.DeviceIdType.MESH
LANES = 128
SUBLANES = 8
RIM = 16
EDGE = RIM // SUBLANES

U, V, A, B, T, Q, GX, GY, C = range(9)


def layout(count):
    deep = 2 * count
    widths = {U: deep, V: deep, A: deep - 1, T: deep - 1, Q: deep - 1}
    for level in range(count):
        widths[C + level] = deep - 1 - 2 * level
    widths.update({B: deep - 2, GX: deep - 2, GY: deep - 2})
    places, at = {}, 0
    for field in widths:
        places[field] = at
        at += widths[field]
    assert at <= LANES
    return widths, places


def spin(cells, shift):
    shift = shift % LANES
    return cells if shift == 0 else pltpu.roll(cells, shift, 1)


def kernel(
    count,
    lats,
    lons,
    route,
    state,
    forcing,
    strength,
    mask,
    regime,
    flux,
    blocks,
    ext,
    raw_stress,
    raw_force,
    raw_strength,
    raw_mask,
    raw_regime,
    pack_west,
    pack_east,
    rim_east,
    rim_west,
    work_u,
    work_v,
    work_a,
    work_b,
    work_t,
    edge,
    outbox,
    order,
    load_sem,
    rim_send,
    rim_recv,
    route_send,
    route_recv,
    own_sem,
):
    fields = C + count
    widths, places = layout(count)
    groups = state.shape[1]
    rows = groups * SUBLANES
    block_rows = rows // lats
    span = block_rows + 2 * RIM
    me = lax.axis_index("lat")
    here = lax.axis_index("lon")
    west = lax.rem(here + lons - 1, lons)
    east = lax.rem(here + 1, lons)
    north = lax.rem(me + lats - 1, lats)
    south = lax.rem(me + 1, lats)

    barrier = pltpu.get_barrier_semaphore()
    greeted = 0
    for step in range(1, lats):
        pl.semaphore_signal(
            barrier, inc=1, device_id=(lax.rem(me + step, lats), here), device_id_type=MESH
        )
        greeted += 1
    for lon in (west, east):
        for lat in (north, me, south):
            pl.semaphore_signal(barrier, inc=1, device_id=(lat, lon), device_id_type=MESH)
            greeted += 1

    loads = []

    def load(src, dst):
        copy = pltpu.make_async_copy(src, dst, load_sem.at[len(loads)])
        copy.start()
        loads.append(copy)

    for tile in range(2):
        lanes = pl.ds(tile * LANES, LANES)
        load(state.at[pl.ds(0, 2), :, :, lanes], ext.at[pl.ds(0, 2), tile, pl.ds(EDGE, groups)])
        load(state.at[pl.ds(2, 3), :, :, lanes], raw_stress.at[:, tile])
        load(forcing.at[:, :, :, lanes], raw_force.at[:, tile])
        load(strength.at[:, :, lanes], raw_strength.at[tile])
        load(mask.at[:, :, lanes], raw_mask.at[tile])
        load(regime.at[:, :, :, lanes], raw_regime.at[:, tile])

    for lat in range(lats):
        block = jnp.int32(0)
        for j in range(1, lats):
            apart = route[me, j] - lat
            block = block + j * (1 - lax.div(apart * apart + 63, 64))
        order[lat] = lax.rem(block, lats)
    for copy in loads:
        copy.wait()

    lane = lax.broadcasted_iota(jnp.int32, (8, LANES), 1)

    def prepare(at, _):
        inside = at + EDGE
        packs = []
        for tile in range(2):
            ice = raw_mask[tile, at].astype(jnp.float32)
            firm = ice * raw_strength[tile, at]
            s1 = ice * raw_stress[0, tile, at]
            s2 = ice * raw_stress[1, tile, at]
            push = (STEP_WEIGHT * DAMP) * ice
            low = firm * (KEEP * 0.125)
            made = {
                U: ext[U, tile, inside],
                V: ext[V, tile, inside],
                A: s1 + s2,
                B: s1 - s2,
                T: (2.0 * ice) * raw_stress[2, tile, at],
                Q: firm * (KEEP * 0.5),
                GX: push * (raw_force[0, tile, at] + DRAG_COEF * raw_force[2, tile, at]),
                GY: push * (raw_force[1, tile, at] + DRAG_COEF * raw_force[3, tile, at]),
            }
            for level in range(count):
                stiff = 3.0 - 2.0 * raw_regime[level, tile, at].astype(jnp.float32)
                made[C + level] = low * stiff
            for field in range(A, fields):
                ext[field, tile, inside] = made[field]
            total = None
            for field, place in places.items():
                moved = spin(made[field], place if tile == 0 else place + widths[field])
                total = moved if total is None else jnp.where(lane >= place, moved, total)
            packs.append(total)
        pack_west[at] = packs[0]
        pack_east[at] = packs[1]
        return 0

    lax.fori_loop(0, groups, prepare, 0, unroll=2)

    pl.semaphore_wait(barrier, greeted)

    def rim_copy(index, src, dst, lat, lon):
        return pltpu.make_async_remote_copy(
            src_ref=src,
            dst_ref=dst,
            send_sem=rim_send.at[index],
            recv_sem=rim_recv.at[index],
            device_id=(lat, lon),
            device_id_type=MESH,
        )

    top, middle, bottom = pl.ds(0, EDGE), pl.ds(EDGE, groups), pl.ds(EDGE + groups, EDGE)
    first, last = pl.ds(0, EDGE), pl.ds(groups - EDGE, EDGE)
    first_inside, last_inside = pl.ds(EDGE, EDGE), pl.ds(groups, EDGE)
    sides = [
        rim_copy(0, pack_west, rim_east.at[middle], me, west),
        rim_copy(1, pack_east, rim_west.at[middle], me, east),
    ]
    ups = [
        rim_copy(2, pack_west.at[first], rim_east.at[bottom], north, west),
        rim_copy(3, pack_east.at[first], rim_west.at[bottom], north, east),
        rim_copy(4, ext.at[:, :, first_inside], ext.at[:, :, bottom], north, here),
    ]
    downs = [
        rim_copy(5, pack_west.at[last], rim_east.at[top], south, west),
        rim_copy(6, pack_east.at[last], rim_west.at[top], south, east),
        rim_copy(7, ext.at[:, :, last_inside], ext.at[:, :, top], south, here),
    ]
    for copy in sides:
        copy.start()

    @pl.when(me > 0)
    def _():
        for copy in ups:
            copy.start()

    @pl.when(me < lats - 1)
    def _():
        for copy in downs:
            copy.start()

    def blank(at):
        nothing = jnp.zeros((EDGE, SUBLANES, LANES), jnp.float32)
        rim_east[at] = nothing
        rim_west[at] = nothing
        for field in range(fields):
            for tile in range(2):
                ext[field, tile, at] = nothing

    @pl.when(me == 0)
    def _():
        blank(top)

    @pl.when(me == lats - 1)
    def _():
        blank(bottom)

    for work in (work_u, work_v, work_a, work_b, work_t):
        for tile in range(3):
            work[tile, pl.ds(0, 8), :] = jnp.zeros((8, LANES), jnp.float32)
            work[tile, pl.ds(span + 8, 8), :] = jnp.zeros((8, LANES), jnp.float32)

    for copy in sides:
        copy.wait_recv()

    @pl.when(me < lats - 1)
    def _():
        for copy in ups:
            copy.wait_recv()

    @pl.when(me > 0)
    def _():
        for copy in downs:
            copy.wait_recv()

    moving = {U: work_u, V: work_v, A: work_a, B: work_b, T: work_t}
    right_end = lane == LANES - 1
    left_end = lane == 0

    def across(tiles):
        ahead = [spin(cells, -1) for cells in tiles]
        behind = [spin(cells, 1) for cells in tiles]
        return [
            jnp.where(right_end, ahead[(t + 1) % 3], ahead[t])
            - jnp.where(left_end, behind[(t + 2) % 3], behind[t])
            for t in range(3)
        ]

    core = lax.rem(me, 2)
    chip = me // 2
    chips = lats // 2
    sign = jnp.where(core == 0, 1, chips - 1)

    def partner(step):
        hop = jnp.where((step == 0) | (step == 4), sign, 0)
        hop = jnp.where((step == 1) | (step == 3), 2, hop)
        hop = jnp.where((step == 2) | (step == 5), chips - sign, hop)
        swap = jnp.where((step == 3) | (step == 4) | (step == 5) | (step == 6), 1, 0)
        return lax.rem(chip + hop, chips) * 2 + lax.rem(core + swap, 2)

    def route_copy(step, lat):
        return pltpu.make_async_remote_copy(
            src_ref=outbox.at[lat],
            dst_ref=blocks.at[me],
            send_sem=route_send.at[step],
            recv_sem=route_recv.at[step],
            device_id=(lat, here),
            device_id_type=MESH,
        )

    def subcycles(target):
        base = order[target] * (block_rows // SUBLANES)

        def wide(field, tile, row):
            return ext[field, tile, base + row // SUBLANES]

        for row in range(0, span, 8):
            from_east = rim_east[base + row // SUBLANES]
            from_west = rim_west[base + row // SUBLANES]
            for field, place in places.items():
                cells = jnp.where(
                    lane < LANES // 2,
                    spin(from_east, -place),
                    spin(from_west, -place - widths[field]),
                )
                if field in moving:
                    moving[field][2, pl.ds(row + 8, 8), :] = cells
                else:
                    edge[field, pl.ds(row, 8), :] = cells
            for field, work in moving.items():
                for tile in range(2):
                    work[tile, pl.ds(row + 8, 8), :] = wide(field, tile, row)

        def fixed(field, tile, row):
            return edge[field, pl.ds(row, 8), :] if tile == 2 else wide(field, tile, row)

        for level in range(count):
            reach = 2 * (count - 1 - level)
            low = (RIM - reach - 1) // 8 * 8
            high = -(-(RIM + block_rows + reach + 1) // 8) * 8
            for row in range(low, high, 8):
                at = pl.ds(row + 8, 8)
                over, under = pl.ds(row + 9, 8), pl.ds(row + 7, 8)
                u_x = across([work_u[t, at, :] for t in range(3)])
                v_x = across([work_v[t, at, :] for t in range(3)])
                for t in range(3):
                    u_y = work_u[t, over, :] - work_u[t, under, :]
                    v_y = work_v[t, over, :] - work_v[t, under, :]
                    c = fixed(C + level, t, row)
                    q = fixed(Q, t, row)
                    both = u_x[t] + v_y
                    work_a[t, at, :] = KEEP * work_a[t, at, :] + (c * (both + 2.0 * u_x[t]) - q)
                    work_b[t, at, :] = KEEP * work_b[t, at, :] + (c * (both + 2.0 * v_y) - q)
                    work_t[t, at, :] = KEEP * work_t[t, at, :] + c * (u_y + v_x[t])
            low = (RIM - reach) // 8 * 8
            high = -(-(RIM + block_rows + reach) // 8) * 8
            final = level == count - 1
            for row in range(low, high, 8):
                at = pl.ds(row + 8, 8)
                over, under = pl.ds(row + 9, 8), pl.ds(row + 7, 8)
                here_a = [work_a[t, at, :] for t in range(3)]
                here_t = [work_t[t, at, :] for t in range(3)]
                a_x = across(here_a)
                t_x = across(here_t)
                for t in range(2 if final else 3):
                    u = work_u[t, at, :]
                    v = work_v[t, at, :]
                    f_x = a_x[t] + (work_t[t, over, :] - work_t[t, under, :])
                    f_y = t_x[t] + (work_b[t, over, :] - work_b[t, under, :])
                    gain = jnp.where(fixed(Q, t, row) > 0.0, DAMP, 0.0)
                    turn = STEP_WEIGHT * CORIOLIS
                    push = STEP_WEIGHT * 0.25
                    next_u = gain * (u + (turn * v + push * f_x)) + fixed(GX, t, row)
                    next_v = gain * (v + (push * f_y - turn * u)) + fixed(GY, t, row)
                    if final:
                        here_b = work_b[t, at, :]
                        done = (
                            next_u,
                            next_v,
                            0.5 * (here_a[t] + here_b),
                            0.5 * (here_a[t] - here_b),
                            0.5 * here_t[t],
                        )
                        lanes = pl.ds(t * LANES, LANES)
                        for part, cells in enumerate(done):
                            outbox[target, part, pl.ds(row - RIM, 8), lanes] = cells
                    else:
                        work_u[t, at, :] = next_u
                        work_v[t, at, :] = next_v

    def deliver(step, _):
        lat = partner(step)
        subcycles(lat)

        @pl.when(step < lats - 1)
        def _():
            route_copy(step, lat).start()

        return 0

    lax.fori_loop(0, lats, deliver, 0)

    own = pltpu.make_async_copy(outbox.at[me], blocks.at[me], own_sem)
    own.start()

    def exchange(j, _):
        taker = route[me, j]
        for part in range(block_rows // 8):
            at = pl.ds(part * 8, 8)
            group = j * (block_rows // SUBLANES) + part
            row = pl.multiple_of(group * SUBLANES, SUBLANES)
            for tile in range(2):
                lanes = pl.ds(tile * LANES, LANES)
                icy = ext[Q, tile, group + EDGE] > 0.0
                for axis in range(2):
                    drift = outbox[taker, axis, at, lanes] - raw_force[2 + axis, tile, group]
                    flux[axis, pl.ds(row, 8), lanes] = jnp.where(icy, DRAG_COEF * drift, 0.0)
        return 0

    lax.fori_loop(0, lats, exchange, 0)

    for copy in sides:
        copy.wait_send()

    @pl.when(me > 0)
    def _():
        for copy in ups:
            copy.wait_send()

    @pl.when(me < lats - 1)
    def _():
        for copy in downs:
            copy.wait_send()

    own.wait()

    def settle(step, _):
        route_copy(step, partner(step)).wait()
        return 0

    lax.fori_loop(0, lats - 1, settle, 0)


def per_device(lats, lons, ice_state, ocean_forcing, ice_strength, ice_mask, yield_mask, ice_route):
    count, rows, columns = yield_mask.shape
    block_rows = rows // lats
    span = block_rows + 2 * RIM
    fields = C + count
    f32 = jnp.float32
    hbm = pl.BlockSpec(memory_space=pl.ANY)
    vmem = pl.BlockSpec(memory_space=pltpu.VMEM)
    work = pltpu.VMEM((3, span + 16, LANES), f32)
    dma = pltpu.SemaphoreType.DMA
    groups = rows // SUBLANES

    def grouped(lead, count, kind=f32):
        return pltpu.VMEM(lead + (count, SUBLANES, LANES), kind)

    def split(cells):
        return cells.reshape(cells.shape[:-2] + (groups, SUBLANES, columns))

    return pl.pallas_call(
        functools.partial(kernel, count, lats, lons),
        out_shape=(
            pltpu.VMEM((2, rows, columns), f32),
            pltpu.VMEM((lats, 5, block_rows, columns), f32),
        ),
        in_specs=[pl.BlockSpec(memory_space=pltpu.SMEM)] + [hbm] * 5,
        out_specs=(vmem, vmem),
        scratch_shapes=[
            grouped((fields, 2), groups + 2 * EDGE),
            grouped((3, 2), groups),
            grouped((4, 2), groups),
            grouped((2,), groups),
            grouped((2,), groups, jnp.int32),
            grouped((count, 2), groups, jnp.int32),
            grouped((), groups),
            grouped((), groups),
            grouped((), groups + 2 * EDGE),
            grouped((), groups + 2 * EDGE),
            work,
            work,
            work,
            work,
            work,
            pltpu.VMEM((fields, span, LANES), f32),
            pltpu.VMEM((lats, 5, block_rows, columns), f32),
            pltpu.SMEM((lats,), jnp.int32),
            dma((12,)),
            dma((8,)),
            dma((8,)),
            dma((lats - 1,)),
            dma((lats - 1,)),
            dma,
        ],
        compiler_params=pltpu.CompilerParams(collective_id=0, has_side_effects=True),
        name="ice_step",
    )(
        ice_route,
        split(ice_state),
        split(ocean_forcing),
        split(ice_strength),
        split(ice_mask),
        split(yield_mask),
    )


def solution(mesh):
    return jax.shard_map(
        functools.partial(per_device, mesh.shape["lat"], mesh.shape["lon"]),
        mesh=mesh,
        in_specs=(
            P(None, "lat", "lon"),
            P(None, "lat", "lon"),
            P("lat", "lon"),
            P("lat", "lon"),
            P(None, "lat", "lon"),
            P(),
        ),
        out_specs=(P(None, "lat", "lon"), P("lat", None, None, "lon")),
        check_vma=False,
    )
```

profile of v0, /device:TPU:1, one launch (start us, length us, event | category | flops | bytes accessed | tf_op | source)
XLA Modules:
  0.0 37.6 jit_solution(16682635859237972611)
XLA Ops:
  0.6 35.1 %ice_step.1 = (f32[2,256,256]{2,1,0:T(8,128)S(1)}, f32[8,5,32,256]{3,2,1,0:T(8,128)S(1)}) custom-call(s32[8,8]{1,0:T(8,128)} %route.1, f32[5,32,8,256]{3,2,1,0:T(8,128)} %bitcast.6, f32[4,32,8,256]{3,2,1,0:T(8,128)} %bitcast.7, f32[32,8,256]{2,1,0:T(8,128)} %bitcast.8, s32[32,8,256]{2,1,0:T(8,128)} %bitcast.9, s32[6,32,8,256]{3,2,1,0:T(8,128)} %bitcast.5), custom_call_target="tpu_custom_call" | custom-call | tf_op jit(solution)/shard_map/ice_step/pallas_call | solution.py:433
  35.7 0.8 %copy.10 = f32[2,256,256]{2,1,0:T(8,128)} copy(f32[2,256,256]{2,1,0:T(8,128)S(1)} %get-tuple-element.2) | data formatting | bytes 1048576
  36.5 1.1 %copy.11 = f32[8,5,32,256]{3,2,1,0:T(8,128)} copy(f32[8,5,32,256]{3,2,1,0:T(8,128)S(1)} %get-tuple-element.3) | data formatting | bytes 2621440
where the time goes:
time: 38.1 us; the launch traced here: 37.6 us
  Pallas kernels  35.1 us (92%)
  local copies, waits for them, and re-layouts  1.85 us (5%)
  between operations  0.64 us (2%)
    pallas_call x1, Pallas kernels, per_device(): pl.pallas_call(functools.partial(kernel, count, lats, lons), out_shape=(p...  35.1 us
    unnamed x2, local copies, waits for them, and re-layouts  1.85 us

commit v1 on v0

v1 whole, which is shorter than its diff:
```python
import functools

import jax
import jax.numpy as jnp
from jax import lax
from jax.experimental import pallas as pl
from jax.experimental.pallas import tpu as pltpu
from jax.sharding import PartitionSpec as P

RELAX_RATE = 1.0
STEP_WEIGHT = 0.5
DRAG_COEF = 0.5
CORIOLIS = 0.3

KEEP = 1.0 / (1.0 + RELAX_RATE)
DAMP = 1.0 / (1.0 + STEP_WEIGHT * DRAG_COEF)

MESH = pl.DeviceIdType.MESH
LANES = 128
HALF = LANES // 2
SUBLANES = 8
RIM = 16
EDGE = RIM // SUBLANES

U, V, A, B, T, Q, GX, GY, C = range(9)
MOVING = 5


def layout(count):
    deep = 2 * count
    widths = {U: deep, V: deep, A: deep - 1, T: deep - 1, Q: deep - 1, C: deep - 1}
    widths.update({B: deep - 2, GX: deep - 2, GY: deep - 2})
    for level in range(1, count):
        widths[C + level] = deep - 1 - 2 * level
    names = list(widths)

    def window(start, width):
        return {(start + i) % LANES for i in range(width)}

    def settle(index, to_west, to_east):
        if index == len(names):
            return {}
        width = widths[names[index]]
        for turn in range(LANES - width + 1):
            mine, other = window(turn, width), window(HALF + turn - width, width)
            if mine & to_west or other & to_east:
                continue
            rest = settle(index + 1, to_west | mine, to_east | other)
            if rest is not None:
                return {names[index]: (turn, (HALF + turn - width) % LANES), **rest}
            if index < len(names) - 3:
                return None
        free_west = [p for p in range(LANES - width + 1) if not window(p, width) & to_west]
        free_east = [p for p in range(LANES - width + 1) if not window(p, width) & to_east]
        if not free_west or not free_east:
            return None
        west, east = free_west[0], free_east[0]
        rest = settle(index + 1, to_west | window(west, width), to_east | window(east, width))
        return None if rest is None else {names[index]: (west, east), **rest}

    return widths, settle(0, set(), set())


def spin(cells, shift):
    shift = shift % LANES
    return cells if shift == 0 else pltpu.roll(cells, shift, 1)


def lay(lane, parts):
    parts = sorted(parts, key=lambda part: part[0])
    start, width, cells = parts[-1]
    total = cells if start + width > LANES else parts[0][2]
    for start, width, cells in parts:
        total = jnp.where(lane >= start, cells, total)
    return total


def stress(u_x, u_y, v_x, v_y, a, b, t, c, q):
    both = u_x + v_y
    next_a = KEEP * a + (c * (both + 2.0 * u_x) - q)
    next_b = KEEP * b + (c * (both + 2.0 * v_y) - q)
    return next_a, next_b, KEEP * t + c * (u_y + v_x)


def momentum(u, v, f_x, f_y, q, g_x, g_y):
    gain = jnp.where(q > 0.0, DAMP, 0.0)
    turn, push = STEP_WEIGHT * CORIOLIS, STEP_WEIGHT * 0.25
    next_u = gain * (u + (turn * v + push * f_x)) + g_x
    next_v = gain * (v + (push * f_y - turn * u)) + g_y
    return next_u, next_v


def finish(u, v, a, b, t):
    return u, v, 0.5 * (a + b), 0.5 * (a - b), 0.5 * t


def reaches(count, level, rows):
    reach = 2 * (count - 1 - level)

    def span(extra):
        low = (RIM - reach - extra) // SUBLANES
        high = -(-(RIM + rows + reach + extra) // SUBLANES)
        return range(low, high)

    return span(1), span(0)


def kernel(
    count,
    lats,
    lons,
    route_in,
    state,
    forcing,
    strength,
    mask,
    regime,
    flux,
    blocks,
    raw_state,
    raw_force,
    raw_strength,
    raw_mask,
    raw_regime,
    ext,
    pack_west,
    pack_east,
    rim_east,
    rim_west,
    work_u,
    work_v,
    work_a,
    work_b,
    work_t,
    side_u,
    side_v,
    side_a,
    side_b,
    side_t,
    side_fixed,
    sides,
    outbox,
    side_out,
    side_in,
    route,
    order,
    load_sem,
    rim_send,
    rim_recv,
    route_send,
    route_recv,
    side_send,
    side_recv,
    own_sem,
    ready,
):
    fields = C + count
    widths, places = layout(count)
    groups = state.shape[1]
    rows = groups * SUBLANES
    block_rows = rows // lats
    block_groups = block_rows // SUBLANES
    deep = 2 * count
    me = lax.axis_index("lat")
    here = lax.axis_index("lon")
    west = lax.rem(here + lons - 1, lons)
    east = lax.rem(here + 1, lons)
    north = lax.rem(me + lats - 1, lats)
    south = lax.rem(me + 1, lats)
    odd = lax.rem(here, 2)

    barrier = pltpu.get_barrier_semaphore()
    for step in range(1, lats):
        pl.semaphore_signal(
            barrier, inc=1, device_id=(lax.rem(me + step, lats), here), device_id_type=MESH
        )
    around = [(lat, lon) for lon in (west, east) for lat in (north, me, south)]

    loads = []

    def load(src, dst):
        copy = pltpu.make_async_copy(src, dst, load_sem.at[len(loads)])
        copy.start()
        loads.append(copy)

    def load_groups(at):
        first = len(loads)
        load(state.at[:, at], raw_state.at[:, at])
        load(forcing.at[:, at], raw_force.at[:, at])
        load(strength.at[at], raw_strength.at[at])
        load(mask.at[at], raw_mask.at[at])
        load(regime.at[:, at], raw_regime.at[:, at])
        return loads[first:]

    half = (groups - 2 * EDGE) // 2
    chunks = [
        load_groups(pl.ds(0, EDGE)),
        load_groups(pl.ds(groups - EDGE, EDGE)),
        load_groups(pl.ds(EDGE, half)),
        load_groups(pl.ds(EDGE + half, groups - 2 * EDGE - half)),
    ]
    load(route_in, route)

    lane = lax.broadcasted_iota(jnp.int32, (SUBLANES, LANES), 1)
    right_part = (lane >= HALF // 2) & (lane < HALF)

    def fold(left, right):
        return jnp.where(right_part, spin(right, HALF), left)

    side_moving = (side_u, side_v, side_a, side_b, side_t)

    def side_rows(group):
        row = (group + 1) * SUBLANES
        return pl.ds(row if isinstance(group, int) else pl.multiple_of(row, SUBLANES), SUBLANES)

    def put_side(field, group, cells):
        if field < MOVING:
            side_moving[field][side_rows(group), :] = cells
        else:
            side_fixed[field - MOVING, group] = cells

    def get_side(field, group):
        if field < MOVING:
            return side_moving[field][side_rows(group), :]
        return side_fixed[field - MOVING, group]

    def prepare(at, _):
        made = []
        for tile in range(2):
            lanes = pl.ds(tile * LANES, LANES)
            ice = raw_mask[at, :, lanes].astype(jnp.float32)
            firm = ice * raw_strength[at, :, lanes]
            s1 = ice * raw_state[2, at, :, lanes]
            s2 = ice * raw_state[3, at, :, lanes]
            push = (STEP_WEIGHT * DAMP) * ice
            low = firm * (KEEP * 0.125)
            cells = {
                U: raw_state[0, at, :, lanes],
                V: raw_state[1, at, :, lanes],
                A: s1 + s2,
                B: s1 - s2,
                T: (2.0 * ice) * raw_state[4, at, :, lanes],
                Q: firm * (KEEP * 0.5),
                GX: push * (raw_force[0, at, :, lanes] + DRAG_COEF * raw_force[2, at, :, lanes]),
                GY: push * (raw_force[1, at, :, lanes] + DRAG_COEF * raw_force[3, at, :, lanes]),
            }
            for level in range(count):
                stiff = 3.0 - 2.0 * raw_regime[level, at, :, lanes].astype(jnp.float32)
                cells[C + level] = low * stiff
            for field in range(fields):
                ext[field, tile, at + EDGE] = cells[field]
            made.append(cells)
        to_west, to_east = [], []
        for field, (start, other) in places.items():
            width = widths[field]
            both = fold(made[0][field], made[1][field])
            put_side(field, at + EDGE, both)
            moved = spin(both, start)
            to_west.append((start, width, moved))
            if other != (HALF + start - width) % LANES:
                moved = spin(both, other + width - HALF)
            to_east.append((other, width, moved))
        pack_west[at] = lay(lane, to_west)
        pack_east[at] = lay(lane, to_east)
        return 0

    def copies_done(chunk):
        for copy in chunk:
            copy.wait()

    copies_done(chunks[0] + chunks[1])
    for end in (0, groups - EDGE):
        for group in range(EDGE):
            prepare(end + group, 0)

    def rim_copy(index, src, dst, lat, lon):
        return pltpu.make_async_remote_copy(
            src_ref=src,
            dst_ref=dst,
            send_sem=rim_send.at[index],
            recv_sem=rim_recv.at[index],
            device_id=(lat, lon),
            device_id_type=MESH,
        )

    far = C + sum(1 for level in range(count) if deep - 1 - 2 * level > SUBLANES)
    near_count = fields - far
    top, middle, bottom = pl.ds(0, EDGE), pl.ds(EDGE, groups), pl.ds(EDGE + groups, EDGE)
    first, last = pl.ds(0, EDGE), pl.ds(groups - EDGE, EDGE)
    wide_fields, late_fields = pl.ds(0, far), pl.ds(far, near_count)

    def lat_copy(index, part, src, dst, lat):
        return rim_copy(index, ext.at[part, :, src], ext.at[part, :, dst], lat, here)

    lat_ups = [
        lat_copy(0, wide_fields, pl.ds(EDGE, EDGE), bottom, north),
        lat_copy(1, late_fields, pl.ds(EDGE, 1), pl.ds(EDGE + groups, 1), north),
    ]
    lat_downs = [
        lat_copy(2, wide_fields, pl.ds(groups, EDGE), top, south),
        lat_copy(3, late_fields, pl.ds(groups + EDGE - 1, 1), pl.ds(EDGE - 1, 1), south),
    ]
    lon_both = [
        rim_copy(4, pack_west, rim_east.at[middle], me, west),
        rim_copy(5, pack_east, rim_west.at[middle], me, east),
    ]
    lon_ups = [
        rim_copy(6, pack_west.at[first], rim_east.at[bottom], north, west),
        rim_copy(7, pack_east.at[first], rim_west.at[bottom], north, east),
    ]
    lon_downs = [
        rim_copy(8, pack_west.at[last], rim_east.at[top], south, west),
        rim_copy(9, pack_east.at[last], rim_west.at[top], south, east),
    ]
    has_north, has_south = me > 0, me < lats - 1

    @pl.when(odd == 0)
    def _():
        pl.semaphore_wait(barrier, lats - 1)

    @pl.when(odd == 1)
    def _():
        pl.semaphore_wait(barrier, lats - 1 + len(around))

    @pl.when(has_north)
    def _():
        for copy in lat_ups:
            copy.start()

    @pl.when(has_south)
    def _():
        for copy in lat_downs:
            copy.start()

    @pl.when(odd == 0)
    def _():
        for target in around:
            pl.semaphore_signal(barrier, inc=1, device_id=target, device_id_type=MESH)

    @pl.when(odd == 1)
    def _():
        for target in around:
            pl.semaphore_signal(ready, inc=1, device_id=target, device_id_type=MESH)

    copies_done(chunks[2])
    lax.fori_loop(EDGE, EDGE + half, prepare, 0, unroll=7)
    copies_done(chunks[3])
    lax.fori_loop(EDGE + half, groups - EDGE, prepare, 0, unroll=7)

    @pl.when(odd == 0)
    def _():
        pl.semaphore_wait(ready, len(around))

    for copy in lon_both:
        copy.start()

    @pl.when(has_north)
    def _():
        for copy in lon_ups:
            copy.start()

    @pl.when(has_south)
    def _():
        for copy in lon_downs:
            copy.start()

    loads[-1].wait()
    for lat in range(lats):
        block = jnp.int32(0)
        for j in range(1, lats):
            apart = route[me, j] - lat
            block = block + j * (1 - lax.div(apart * apart + 63, 64))
        order[lat] = lax.rem(block, lats)

    def blank(at):
        nothing = jnp.zeros((EDGE, SUBLANES, LANES), jnp.float32)
        rim_east[at] = nothing
        rim_west[at] = nothing
        for field in range(fields):
            for tile in range(2):
                ext[field, tile, at] = nothing

    @pl.when(me == 0)
    def _():
        blank(top)

    @pl.when(me == lats - 1)
    def _():
        blank(bottom)

    line = jnp.zeros((SUBLANES, LANES), jnp.float32)
    for work in (work_u, work_v, work_a, work_b, work_t):
        for tile in range(2):
            work[tile, pl.ds(0, SUBLANES), :] = line
            work[tile, pl.ds(block_rows + 2 * RIM + SUBLANES, SUBLANES), :] = line
    for side in (side_u, side_v, side_a, side_b, side_t):
        side[pl.ds(0, SUBLANES), :] = line
        side[pl.ds(rows + 2 * RIM + SUBLANES, SUBLANES), :] = line

    @pl.when(has_south)
    def _():
        for copy in lat_ups:
            copy.wait_recv()

    @pl.when(has_north)
    def _():
        for copy in lat_downs:
            copy.wait_recv()

    core = lax.rem(me, 2)
    chip = me // 2
    chips = lats // 2

    def hop_of(step, core):
        sign = jnp.where(core == 0, 1, chips - 1)
        hop = jnp.where((step == 0) | (step == 4), sign, 0)
        hop = jnp.where((step == 1) | (step == 3), 2, hop)
        return jnp.where((step == 2) | (step == 5), chips - sign, hop)

    def swap_of(step):
        return jnp.where((step >= 3) & (step <= 6), 1, 0)

    def taker_of(step):
        lat_chip = lax.rem(chip + hop_of(step, core), chips)
        return lat_chip * 2 + lax.rem(core + swap_of(step), 2)

    def giver_of(step):
        other = lax.rem(core + swap_of(step), 2)
        return lax.rem(chip + chips - hop_of(step, other), chips) * 2 + other

    def route_copy(step, lat, slot):
        return pltpu.make_async_remote_copy(
            src_ref=outbox.at[lat],
            dst_ref=blocks.at[slot],
            send_sem=route_send.at[step],
            recv_sem=route_recv.at[step],
            device_id=(lat, here),
            device_id_type=MESH,
        )

    def side_copy(step, lat, slot):
        return pltpu.make_async_remote_copy(
            src_ref=side_out.at[lat],
            dst_ref=side_in.at[slot],
            send_sem=side_send.at[step],
            recv_sem=side_recv.at[step],
            device_id=(lat, here),
            device_id_type=MESH,
        )

    right_end = lane == LANES - 1
    left_end = lane == 0

    def across(tiles):
        ahead = [spin(cells, -1) for cells in tiles]
        behind = [spin(cells, 1) for cells in tiles]
        return [
            jnp.where(right_end, ahead[1 - t], ahead[t])
            - jnp.where(left_end, behind[1 - t], behind[t])
            for t in range(2)
        ]

    def around_row(group):
        row = (group + 1) * SUBLANES
        return [pl.ds(row + shift, SUBLANES) for shift in (0, 1, -1)]

    def subcycles(target):
        base = order[target] * block_groups

        def fixed(field, tile, group):
            return ext[field, tile, base + group]

        for group in range(block_groups + 2 * EDGE):
            at = around_row(group)[0]
            for tile in range(2):
                work_u[tile, at, :] = fixed(U, tile, group)
                work_v[tile, at, :] = fixed(V, tile, group)

        for level in range(count):
            stress_span, momentum_span = reaches(count, level, block_rows)
            for group in stress_span:
                at, over, under = around_row(group)
                u_x = across([work_u[t, at, :] for t in range(2)])
                v_x = across([work_v[t, at, :] for t in range(2)])
                for t in range(2):
                    u_y = work_u[t, over, :] - work_u[t, under, :]
                    v_y = work_v[t, over, :] - work_v[t, under, :]
                    if level == 0:
                        old = [fixed(field, t, group) for field in (A, B, T)]
                    else:
                        old = [work[t, at, :] for work in (work_a, work_b, work_t)]
                    c, q = fixed(C + level, t, group), fixed(Q, t, group)
                    new = stress(u_x[t], u_y, v_x[t], v_y, *old, c, q)
                    for work, cells in zip((work_a, work_b, work_t), new):
                        work[t, at, :] = cells
            final = level == count - 1
            for group in momentum_span:
                at, over, under = around_row(group)
                here_a = [work_a[t, at, :] for t in range(2)]
                here_t = [work_t[t, at, :] for t in range(2)]
                a_x, t_x = across(here_a), across(here_t)
                for t in range(2):
                    f_x = a_x[t] + (work_t[t, over, :] - work_t[t, under, :])
                    f_y = t_x[t] + (work_b[t, over, :] - work_b[t, under, :])
                    new = momentum(
                        work_u[t, at, :],
                        work_v[t, at, :],
                        f_x,
                        f_y,
                        fixed(Q, t, group),
                        fixed(GX, t, group),
                        fixed(GY, t, group),
                    )
                    if final:
                        done = finish(*new, here_a[t], work_b[t, at, :], here_t[t])
                        inside = pl.ds((group - EDGE) * SUBLANES, SUBLANES)
                        for part, cells in enumerate(done):
                            outbox[target, part, inside, pl.ds(t * LANES, LANES)] = cells
                    else:
                        work_u[t, at, :], work_v[t, at, :] = new

    def deliver(step, _):
        lat = taker_of(step)
        subcycles(lat)

        @pl.when(step < lats - 1)
        def _():
            route_copy(step, lat, me).start()

        return 0

    lax.fori_loop(0, lats - 2, deliver, 0)

    for copy in lon_both:
        copy.wait_recv()

    @pl.when(has_south)
    def _():
        for copy in lon_ups:
            copy.wait_recv()

    @pl.when(has_north)
    def _():
        for copy in lon_downs:
            copy.wait_recv()

    def unpack(group, names, beyond):
        from_east, from_west = rim_east[group], rim_west[group]
        for field in names:
            start, other = places[field]
            width = widths[field]
            if other == (HALF + start - width) % LANES:
                end = (start + HALF // 2) % LANES
                if start < end:
                    mine = (lane >= start) & (lane < end)
                else:
                    mine = (lane >= start) | (lane < end)
                rim = spin(jnp.where(mine, from_east, from_west), HALF - start)
            else:
                rim = jnp.where(
                    lane < LANES - HALF // 2,
                    spin(from_east, HALF - start),
                    spin(from_west, -other - width),
                )
            if beyond:
                base = fold(ext[field, 0, group], ext[field, 1, group])
            else:
                base = get_side(field, group)
            put_side(field, group, jnp.where(lane < HALF, base, rim))

    for group in (0, groups + 2 * EDGE - 1):
        unpack(group, range(far), True)
    for group in (1, groups + 2 * EDGE - 2):
        unpack(group, range(fields), True)

    def unpack_inside(group, _):
        unpack(group, range(fields), False)
        return 0

    lax.fori_loop(EDGE, groups + EDGE, unpack_inside, 0, unroll=8)

    def beside(cells):
        return spin(cells, -1) - spin(cells, 1)

    def middle_of(part):
        return 2 * deep * part + deep

    for level in range(count):
        stress_span, momentum_span = reaches(count, level, rows)
        for group in stress_span:
            at, over, under = around_row(group)
            new = stress(
                beside(side_u[at, :]),
                side_u[over, :] - side_u[under, :],
                beside(side_v[at, :]),
                side_v[over, :] - side_v[under, :],
                side_a[at, :],
                side_b[at, :],
                side_t[at, :],
                side_fixed[C + level - MOVING, group],
                side_fixed[Q - MOVING, group],
            )
            side_a[at, :], side_b[at, :], side_t[at, :] = new
        for group in momentum_span:
            at, over, under = around_row(group)
            a, b, t = side_a[at, :], side_b[at, :], side_t[at, :]
            new = momentum(
                side_u[at, :],
                side_v[at, :],
                beside(a) + (side_t[over, :] - side_t[under, :]),
                beside(t) + (side_b[over, :] - side_b[under, :]),
                side_fixed[Q - MOVING, group],
                side_fixed[GX - MOVING, group],
                side_fixed[GY - MOVING, group],
            )
            if level < count - 1:
                side_u[at, :], side_v[at, :] = new
            else:
                parts = []
                for part, cells in enumerate(finish(*new, a, b, t)):
                    cells = jnp.where(lane < HALF // 2, cells, spin(cells, HALF))
                    start = middle_of(part) - deep
                    parts.append((start, 2 * deep, spin(cells, middle_of(part))))
                sides[group - EDGE] = lay(lane, parts)

    def deliver_sides(step, _):
        lat = taker_of(step)
        base = order[lat] * block_groups
        for group in range(block_groups):
            side_out[lat, group] = sides[base + group]

        @pl.when(step < lats - 1)
        def _():
            side_copy(step, lat, me).start()

        return 0

    lax.fori_loop(0, lats, deliver_sides, 0)
    lax.fori_loop(lats - 2, lats, deliver, 0)

    own = pltpu.make_async_copy(outbox.at[me], blocks.at[me], own_sem)
    own.start()

    def place(packed, part, tiles):
        moved = spin(packed, -middle_of(part))
        return (
            jnp.where(lane < deep, moved, tiles[0]),
            jnp.where(lane >= LANES - deep, moved, tiles[1]),
        )

    both_lanes = [pl.ds(tile * LANES, LANES) for tile in range(2)]

    def exchange(j, _):
        taker = route[me, j]
        for part in range(block_groups):
            at = pl.ds(part * SUBLANES, SUBLANES)
            group = j * block_groups + part
            row = pl.multiple_of(group * SUBLANES, SUBLANES)
            for axis in range(2):
                drift = [outbox[taker, axis, at, lanes] for lanes in both_lanes]
                drift = place(sides[group], axis, drift)
                for tile, lanes in enumerate(both_lanes):
                    icy = ext[Q, tile, group + EDGE] > 0.0
                    moved = drift[tile] - raw_force[2 + axis, group, :, lanes]
                    flux[axis, pl.ds(row, SUBLANES), lanes] = jnp.where(icy, DRAG_COEF * moved, 0.0)
        return 0

    lax.fori_loop(0, lats, exchange, 0)

    def mend(slot, source):
        for group in range(block_groups):
            packed = source[slot, group]
            at = pl.ds(group * SUBLANES, SUBLANES)
            for part in range(MOVING):
                tiles = place(packed, part, [blocks[slot, part, at, lanes] for lanes in both_lanes])
                for lanes, cells in zip(both_lanes, tiles):
                    blocks[slot, part, at, lanes] = cells

    own.wait()
    mend(me, side_out)

    def receive(step, _):
        lat = giver_of(step)
        route_copy(step, lat, lat).wait_recv()
        side_copy(step, lat, lat).wait_recv()
        mend(lat, side_in)
        return 0

    lax.fori_loop(0, lats - 1, receive, 0)

    def settle(step, _):
        route_copy(step, taker_of(step), me).wait_send()
        side_copy(step, taker_of(step), me).wait_send()
        return 0

    lax.fori_loop(0, lats - 1, settle, 0)

    for copy in lon_both:
        copy.wait_send()

    @pl.when(has_north)
    def _():
        for copy in lat_ups + lon_ups:
            copy.wait_send()

    @pl.when(has_south)
    def _():
        for copy in lat_downs + lon_downs:
            copy.wait_send()


def per_device(lats, lons, ice_state, ocean_forcing, ice_strength, ice_mask, yield_mask, ice_route):
    count, rows, columns = yield_mask.shape
    block_rows = rows // lats
    fields = C + count
    groups = rows // SUBLANES
    f32, i32 = jnp.float32, jnp.int32
    hbm = pl.BlockSpec(memory_space=pl.ANY)
    vmem = pl.BlockSpec(memory_space=pltpu.VMEM)
    dma = pltpu.SemaphoreType.DMA

    def tiles(*lead, kind=f32, wide=LANES):
        return pltpu.VMEM(lead + (SUBLANES, wide), kind)

    def split(cells):
        return cells.reshape(cells.shape[:-2] + (groups, SUBLANES, columns))

    work = pltpu.VMEM((2, block_rows + 2 * RIM + 2 * SUBLANES, LANES), f32)
    side = pltpu.VMEM((rows + 2 * RIM + 2 * SUBLANES, LANES), f32)
    return pl.pallas_call(
        functools.partial(kernel, count, lats, lons),
        out_shape=(
            pltpu.VMEM((2, rows, columns), f32),
            pltpu.VMEM((lats, 5, block_rows, columns), f32),
        ),
        in_specs=[hbm] * 6,
        out_specs=(vmem, vmem),
        scratch_shapes=[
            tiles(5, groups, wide=columns),
            tiles(4, groups, wide=columns),
            tiles(groups, wide=columns),
            tiles(groups, kind=i32, wide=columns),
            tiles(count, groups, kind=i32, wide=columns),
            tiles(fields, 2, groups + 2 * EDGE),
            tiles(groups),
            tiles(groups),
            tiles(groups + 2 * EDGE),
            tiles(groups + 2 * EDGE),
            work,
            work,
            work,
            work,
            work,
            side,
            side,
            side,
            side,
            side,
            tiles(fields - MOVING, groups + 2 * EDGE),
            tiles(groups),
            pltpu.VMEM((lats, 5, block_rows, columns), f32),
            tiles(lats, block_rows // SUBLANES),
            tiles(lats, block_rows // SUBLANES),
            pltpu.SMEM((lats, lats), i32),
            pltpu.SMEM((lats,), i32),
            dma((21,)),
            dma((10,)),
            dma((10,)),
            dma((lats - 1,)),
            dma((lats - 1,)),
            dma((lats - 1,)),
            dma((lats - 1,)),
            dma,
            pltpu.SemaphoreType.REGULAR,
        ],
        compiler_params=pltpu.CompilerParams(collective_id=0, has_side_effects=True),
        name="ice_step",
    )(
        ice_route,
        split(ice_state),
        split(ocean_forcing),
        split(ice_strength),
        split(ice_mask),
        split(yield_mask),
    )


def solution(mesh):
    return jax.shard_map(
        functools.partial(per_device, mesh.shape["lat"], mesh.shape["lon"]),
        mesh=mesh,
        in_specs=(
            P(None, "lat", "lon"),
            P(None, "lat", "lon"),
            P("lat", "lon"),
            P("lat", "lon"),
            P(None, "lat", "lon"),
            P(),
        ),
        out_specs=(P(None, "lat", "lon"), P("lat", None, None, "lon")),
        check_vma=False,
    )
```

time: 38.1 us -> 35.5 us (0.932); the launches traced: 37.6 us -> 35.4 us
  Pallas kernels: 35.1 us -> 32.9 us
    pallas_call x1, Pallas kernels: 35.1 us -> 32.9 us  [per_device(): pl.pallas_call(functools.partial(kernel, count, lats, lons), out_shape=(p...]
where the time goes in v1:
time: 35.5 us; the launch traced here: 35.4 us
  Pallas kernels  32.9 us (93%)
  local copies, waits for them, and re-layouts  1.85 us (5%)
  between operations  0.64 us (2%)
    pallas_call x1, Pallas kernels, per_device(): pl.pallas_call(functools.partial(kernel, count, lats, lons), out_shape=(p...  32.9 us
    unnamed x2, local copies, waits for them, and re-layouts  1.85 us

profile of v1, /device:TPU:1, one launch (start us, length us, event | category | flops | bytes accessed | tf_op | source)
XLA Modules:
  0.0 35.4 jit_solution(9671564585746793400)
XLA Ops:
  0.6 32.9 %ice_step.1 = (f32[2,256,256]{2,1,0:T(8,128)S(1)}, f32[8,5,32,256]{3,2,1,0:T(8,128)S(1)}) custom-call(s32[8,8]{1,0:T(8,128)} %route_in.1, f32[5,32,8,256]{3,2,1,0:T(8,128)} %bitcast.6, f32[4,32,8,256]{3,2,1,0:T(8,128)} %bitcast.7, f32[32,8,256]{2,1,0:T(8,128)} %bitcast.8, s32[32,8,256]{2,1,0:T(8,128)} %bitcast.9, s32[6,32,8,256]{3,2,1,0:T(8,128)} %bitcast.5), custom_call_target="tpu_custom_call" | custom-call | tf_op jit(solution)/shard_map/ice_step/pallas_call | solution.py:730
  33.6 0.8 %copy.10 = f32[2,256,256]{2,1,0:T(8,128)} copy(f32[2,256,256]{2,1,0:T(8,128)S(1)} %get-tuple-element.2) | data formatting | bytes 1048576
  34.4 1.1 %copy.11 = f32[8,5,32,256]{3,2,1,0:T(8,128)} copy(f32[8,5,32,256]{3,2,1,0:T(8,128)S(1)} %get-tuple-element.3) | data formatting | bytes 2621440

commit v2 on v1

--- a/solution.py
+++ b/solution.py
@@ -519,11 +519,13 @@
                     else:
                         work_u[t, at, :], work_v[t, at, :] = new
 
+    held = lats - 3
+
     def deliver(step, _):
         lat = taker_of(step)
         subcycles(lat)
 
-        @pl.when(step < lats - 1)
+        @pl.when((step < lats - 1) & (step != held))
         def _():
             route_copy(step, lat, me).start()
 
@@ -636,6 +638,7 @@
         return 0
 
     lax.fori_loop(0, lats, deliver_sides, 0)
+    route_copy(held, taker_of(held), me).start()
     lax.fori_loop(lats - 2, lats, deliver, 0)
 
     own = pltpu.make_async_copy(outbox.at[me], blocks.at[me], own_sem)
@@ -679,7 +682,8 @@
     own.wait()
     mend(me, side_out)
 
-    def receive(step, _):
+    def receive(turn, _):
+        step = jnp.where(turn < held, turn, jnp.where(turn == held, held + 1, held))
         lat = giver_of(step)
         route_copy(step, lat, lat).wait_recv()
         side_copy(step, lat, lat).wait_recv()
@@ -707,6 +711,17 @@
     def _():
         for copy in lat_downs + lon_downs:
             copy.wait_send()
+
+
+def hand_out(flux, blocks, flux_out, blocks_out, sems):
+    copies = [
+        pltpu.make_async_copy(flux, flux_out, sems.at[0]),
+        pltpu.make_async_copy(blocks, blocks_out, sems.at[1]),
+    ]
+    for copy in copies:
+        copy.start()
+    for copy in copies:
+        copy.wait()
 
 
 def per_device(lats, lons, ice_state, ocean_forcing, ice_strength, ice_mask, yield_mask, ice_route):
@@ -715,7 +730,7 @@
     fields = C + count
     groups = rows // SUBLANES
     f32, i32 = jnp.float32, jnp.int32
-    hbm = pl.BlockSpec(memory_space=pl.ANY)
+    as_is = pl.BlockSpec(memory_space=pl.ANY)
     vmem = pl.BlockSpec(memory_space=pltpu.VMEM)
     dma = pltpu.SemaphoreType.DMA
 
@@ -727,13 +742,11 @@
 
     work = pltpu.VMEM((2, block_rows + 2 * RIM + 2 * SUBLANES, LANES), f32)
     side = pltpu.VMEM((rows + 2 * RIM + 2 * SUBLANES, LANES), f32)
-    return pl.pallas_call(
+    shapes = ((2, rows, columns), (lats, 5, block_rows, columns))
+    results = pl.pallas_call(
         functools.partial(kernel, count, lats, lons),
-        out_shape=(
-            pltpu.VMEM((2, rows, columns), f32),
-            pltpu.VMEM((lats, 5, block_rows, columns), f32),
-        ),
-        in_specs=[hbm] * 6,
+        out_shape=tuple(pltpu.VMEM(shape, f32) for shape in shapes),
+        in_specs=[as_is] * 6,
         out_specs=(vmem, vmem),
         scratch_shapes=[
             tiles(5, groups, wide=columns),
@@ -783,6 +796,15 @@
         split(ice_mask),
         split(yield_mask),
     )
+    return pl.pallas_call(
+        hand_out,
+        out_shape=tuple(jax.ShapeDtypeStruct(shape, f32) for shape in shapes),
+        in_specs=[as_is] * 2,
+        out_specs=(as_is, as_is),
+        scratch_shapes=[dma((2,))],
+        compiler_params=pltpu.CompilerParams(vmem_limit_bytes=1 << 20),
+        name="hand_out",
+    )(*results)
 
 
 def solution(mesh):

time: 35.5 us -> 33.7 us (0.949)
  local copies, waits for them, and re-layouts: 1.85 us -> 0 us
    unnamed x2 -> x0, local copies, waits for them, and re-layouts: 1.85 us -> none
    pallas_call x1 -> x2, Pallas kernels: 32.9 us -> 32.8 us  [the longest x1 31.5 us: per_device(): pl.pallas_call(functools.partial(kernel, count, lats, lons), out_shape=tu...]
where the time goes in v2:
time: 33.7 us; the launch traced here: 33.4 us
  Pallas kernels  32.8 us (97%)
  between operations  0.64 us (2%)
    pallas_call x1, Pallas kernels, per_device(): pl.pallas_call(functools.partial(kernel, count, lats, lons), out_shape=tu...  31.5 us
    pallas_call x1, Pallas kernels, per_device(): pl.pallas_call(hand_out, out_shape=tuple((jax.ShapeDtypeStruct(shape, f32...  1.25 us

profile of v2, /device:TPU:1, one launch (start us, length us, event | category | flops | bytes accessed | tf_op | source)
XLA Modules:
  0.0 33.4 jit_solution(6176689087676164742)
XLA Ops:
  0.6 31.5 %ice_step.1 = (f32[2,256,256]{2,1,0:T(8,128)S(1)}, f32[8,5,32,256]{3,2,1,0:T(8,128)S(1)}) custom-call(s32[8,8]{1,0:T(8,128)} %route_in.1, f32[5,32,8,256]{3,2,1,0:T(8,128)} %bitcast.6, f32[4,32,8,256]{3,2,1,0:T(8,128)} %bitcast.7, f32[32,8,256]{2,1,0:T(8,128)} %bitcast.8, s32[32,8,256]{2,1,0:T(8,128)} %bitcast.9, s32[6,32,8,256]{3,2,1,0:T(8,128)} %bitcast.5), custom_call_target="tpu_custom_call" | custom-call | tf_op jit(solution)/shard_map/ice_step/pallas_call | solution.py:746
  32.2 1.2 %hand_out.1 = (f32[2,256,256]{2,1,0:T(8,128)}, f32[8,5,32,256]{3,2,1,0:T(8,128)}) custom-call(f32[2,256,256]{2,1,0:T(8,128)S(1)} %get-tuple-element.4.flux, f32[8,5,32,256]{3,2,1,0:T(8,128)S(1)} %get-tuple-element.5.blocks), custom_call_target="tpu_custom_call" | custom-call | tf_op jit(solution)/shard_map/hand_out/pallas_call | solution.py:799

commit v3 on v2

--- a/solution.py
+++ b/solution.py
@@ -285,7 +285,7 @@
 
     far = C + sum(1 for level in range(count) if deep - 1 - 2 * level > SUBLANES)
     near_count = fields - far
-    top, middle, bottom = pl.ds(0, EDGE), pl.ds(EDGE, groups), pl.ds(EDGE + groups, EDGE)
+    top, bottom = pl.ds(0, EDGE), pl.ds(EDGE + groups, EDGE)
     first, last = pl.ds(0, EDGE), pl.ds(groups - EDGE, EDGE)
     wide_fields, late_fields = pl.ds(0, far), pl.ds(far, near_count)
 
@@ -300,10 +300,17 @@
         lat_copy(2, wide_fields, pl.ds(groups, EDGE), top, south),
         lat_copy(3, late_fields, pl.ds(groups + EDGE - 1, 1), pl.ds(EDGE - 1, 1), south),
     ]
-    lon_both = [
-        rim_copy(4, pack_west, rim_east.at[middle], me, west),
-        rim_copy(5, pack_east, rim_west.at[middle], me, east),
-    ]
+
+    def lon_copies(index, start, size):
+        src, dst = pl.ds(start, size), pl.ds(start + EDGE, size)
+        return [
+            rim_copy(index, pack_west.at[src], rim_east.at[dst], me, west),
+            rim_copy(index + 1, pack_east.at[src], rim_west.at[dst], me, east),
+        ]
+
+    lon_early = lon_copies(4, 0, EDGE + half)
+    lon_late = lon_copies(10, EDGE + half, groups - EDGE - half)
+    lon_both = lon_early + lon_late
     lon_ups = [
         rim_copy(6, pack_west.at[first], rim_east.at[bottom], north, west),
         rim_copy(7, pack_east.at[first], rim_west.at[bottom], north, east),
@@ -342,27 +349,35 @@
         for target in around:
             pl.semaphore_signal(ready, inc=1, device_id=target, device_id_type=MESH)
 
+    def send_lon(part):
+        for copy in part:
+            copy.start()
+
     copies_done(chunks[2])
     lax.fori_loop(EDGE, EDGE + half, prepare, 0, unroll=7)
+
+    @pl.when(odd == 1)
+    def _():
+        send_lon(lon_early)
+
     copies_done(chunks[3])
     lax.fori_loop(EDGE + half, groups - EDGE, prepare, 0, unroll=7)
 
-    @pl.when(odd == 0)
-    def _():
-        pl.semaphore_wait(ready, len(around))
-
-    for copy in lon_both:
-        copy.start()
-
-    @pl.when(has_north)
-    def _():
-        for copy in lon_ups:
-            copy.start()
-
-    @pl.when(has_south)
-    def _():
-        for copy in lon_downs:
-            copy.start()
+    def send_corners():
+        @pl.when(has_north)
+        def _():
+            for copy in lon_ups:
+                copy.start()
+
+        @pl.when(has_south)
+        def _():
+            for copy in lon_downs:
+                copy.start()
+
+    @pl.when(odd == 1)
+    def _():
+        send_lon(lon_late)
+        send_corners()
 
     loads[-1].wait()
     for lat in range(lats):
@@ -521,8 +536,17 @@
 
     held = lats - 3
 
+    answered = 2
+
     def deliver(step, _):
         lat = taker_of(step)
+
+        @pl.when((odd == 0) & (step == answered))
+        def _():
+            pl.semaphore_wait(ready, len(around))
+            send_lon(lon_both)
+            send_corners()
+
         subcycles(lat)
 
         @pl.when((step < lats - 1) & (step != held))
@@ -777,8 +801,8 @@
             pltpu.SMEM((lats, lats), i32),
             pltpu.SMEM((lats,), i32),
             dma((21,)),
-            dma((10,)),
-            dma((10,)),
+            dma((12,)),
+            dma((12,)),
             dma((lats - 1,)),
             dma((lats - 1,)),
             dma((lats - 1,)),

time: 33.7 us -> 32.5 us (0.964)
  the two profiles are of different devices: /device:TPU:1 before, /device:TPU:2 now
where the time goes in v3:
time: 32.5 us; the launch traced here: 32.4 us
  Pallas kernels  31.7 us (98%)
  between operations  0.64 us (2%)
    pallas_call x1, Pallas kernels, per_device(): pl.pallas_call(functools.partial(kernel, count, lats, lons), out_shape=tu...  30.5 us
    pallas_call x1, Pallas kernels, per_device(): pl.pallas_call(hand_out, out_shape=tuple((jax.ShapeDtypeStruct(shape, f32...  1.25 us

profile of v3, /device:TPU:2, one launch (start us, length us, event | category | flops | bytes accessed | tf_op | source)
XLA Modules:
  0.0 32.4 jit_solution(10911726945474019087)
XLA Ops:
  0.6 30.5 %ice_step.1 = (f32[2,256,256]{2,1,0:T(8,128)S(1)}, f32[8,5,32,256]{3,2,1,0:T(8,128)S(1)}) custom-call(s32[8,8]{1,0:T(8,128)} %route_in.1, f32[5,32,8,256]{3,2,1,0:T(8,128)} %bitcast.6, f32[4,32,8,256]{3,2,1,0:T(8,128)} %bitcast.7, f32[32,8,256]{2,1,0:T(8,128)} %bitcast.8, s32[32,8,256]{2,1,0:T(8,128)} %bitcast.9, s32[6,32,8,256]{3,2,1,0:T(8,128)} %bitcast.5), custom_call_target="tpu_custom_call" | custom-call | tf_op jit(solution)/shard_map/ice_step/pallas_call | solution.py:770
  31.1 1.2 %hand_out.1 = (f32[2,256,256]{2,1,0:T(8,128)}, f32[8,5,32,256]{3,2,1,0:T(8,128)}) custom-call(f32[2,256,256]{2,1,0:T(8,128)S(1)} %get-tuple-element.4.flux, f32[8,5,32,256]{3,2,1,0:T(8,128)S(1)} %get-tuple-element.5.blocks), custom_call_target="tpu_custom_call" | custom-call | tf_op jit(solution)/shard_map/hand_out/pallas_call | solution.py:823

commit v4 on v3

--- a/solution.py
+++ b/solution.py
@@ -21,6 +21,7 @@
 SUBLANES = 8
 RIM = 16
 EDGE = RIM // SUBLANES
+HELD = 1
 
 U, V, A, B, T, Q, GX, GY, C = range(9)
 MOVING = 5
@@ -534,7 +535,8 @@
                     else:
                         work_u[t, at, :], work_v[t, at, :] = new
 
-    held = lats - 3
+    partner_step = lats - 2
+    held = range(partner_step - HELD, partner_step)
 
     answered = 2
 
@@ -549,7 +551,7 @@
 
         subcycles(lat)
 
-        @pl.when((step < lats - 1) & (step != held))
+        @pl.when((step < held[0]) | (step == partner_step))
         def _():
             route_copy(step, lat, me).start()
 
@@ -655,18 +657,13 @@
         for group in range(block_groups):
             side_out[lat, group] = sides[base + group]
 
-        @pl.when(step < lats - 1)
+        @pl.when((step < held[0]) | (step == partner_step))
         def _():
             side_copy(step, lat, me).start()
 
         return 0
 
     lax.fori_loop(0, lats, deliver_sides, 0)
-    route_copy(held, taker_of(held), me).start()
-    lax.fori_loop(lats - 2, lats, deliver, 0)
-
-    own = pltpu.make_async_copy(outbox.at[me], blocks.at[me], own_sem)
-    own.start()
 
     def place(packed, part, tiles):
         moved = spin(packed, -middle_of(part))
@@ -676,6 +673,23 @@
         )
 
     both_lanes = [pl.ds(tile * LANES, LANES) for tile in range(2)]
+
+    def mend(whole, slot, source):
+        for group in range(block_groups):
+            packed = source[slot, group]
+            at = pl.ds(group * SUBLANES, SUBLANES)
+            for part in range(MOVING):
+                tiles = place(packed, part, [whole[slot, part, at, lanes] for lanes in both_lanes])
+                for lanes, cells in zip(both_lanes, tiles):
+                    whole[slot, part, at, lanes] = cells
+
+    for step in held:
+        mend(outbox, taker_of(step), side_out)
+        route_copy(step, taker_of(step), me).start()
+    lax.fori_loop(lats - 2, lats, deliver, 0)
+
+    own = pltpu.make_async_copy(outbox.at[me], blocks.at[me], own_sem)
+    own.start()
 
     def exchange(j, _):
         taker = route[me, j]
@@ -694,34 +708,30 @@
 
     lax.fori_loop(0, lats, exchange, 0)
 
-    def mend(slot, source):
-        for group in range(block_groups):
-            packed = source[slot, group]
-            at = pl.ds(group * SUBLANES, SUBLANES)
-            for part in range(MOVING):
-                tiles = place(packed, part, [blocks[slot, part, at, lanes] for lanes in both_lanes])
-                for lanes, cells in zip(both_lanes, tiles):
-                    blocks[slot, part, at, lanes] = cells
-
     own.wait()
-    mend(me, side_out)
+    mend(blocks, me, side_out)
 
     def receive(turn, _):
-        step = jnp.where(turn < held, turn, jnp.where(turn == held, held + 1, held))
+        step = jnp.where(turn < held[0], turn, partner_step)
         lat = giver_of(step)
         route_copy(step, lat, lat).wait_recv()
         side_copy(step, lat, lat).wait_recv()
-        mend(lat, side_in)
+        mend(blocks, lat, side_in)
         return 0
 
-    lax.fori_loop(0, lats - 1, receive, 0)
-
-    def settle(step, _):
+    lax.fori_loop(0, held[0] + 1, receive, 0)
+    for step in held:
+        route_copy(step, giver_of(step), giver_of(step)).wait_recv()
+
+    def settle(turn, _):
+        step = jnp.where(turn < held[0], turn, partner_step)
         route_copy(step, taker_of(step), me).wait_send()
         side_copy(step, taker_of(step), me).wait_send()
         return 0
 
-    lax.fori_loop(0, lats - 1, settle, 0)
+    lax.fori_loop(0, held[0] + 1, settle, 0)
+    for step in held:
+        route_copy(step, taker_of(step), me).wait_send()
 
     for copy in lon_both:
         copy.wait_send()

time: 32.5 us -> 32.2 us (level)
  no operation moved by 1% of the time
where the time goes in v4:
time: 32.2 us; the launch traced here: 32.1 us
  Pallas kernels  31.5 us (98%)
  between operations  0.64 us (2%)
    pallas_call x1, Pallas kernels, per_device(): pl.pallas_call(functools.partial(kernel, count, lats, lons), out_shape=tu...  30.2 us
    pallas_call x1, Pallas kernels, per_device(): pl.pallas_call(hand_out, out_shape=tuple((jax.ShapeDtypeStruct(shape, f32...  1.25 us

profile of v4, /device:TPU:2, one launch (start us, length us, event | category | flops | bytes accessed | tf_op | source)
XLA Modules:
  0.0 32.1 jit_solution(12566800538766006572)
XLA Ops:
  0.6 30.2 %ice_step.1 = (f32[2,256,256]{2,1,0:T(8,128)S(1)}, f32[8,5,32,256]{3,2,1,0:T(8,128)S(1)}) custom-call(s32[8,8]{1,0:T(8,128)} %route_in.1, f32[5,32,8,256]{3,2,1,0:T(8,128)} %bitcast.6, f32[4,32,8,256]{3,2,1,0:T(8,128)} %bitcast.7, f32[32,8,256]{2,1,0:T(8,128)} %bitcast.8, s32[32,8,256]{2,1,0:T(8,128)} %bitcast.9, s32[6,32,8,256]{3,2,1,0:T(8,128)} %bitcast.5), custom_call_target="tpu_custom_call" | custom-call | tf_op jit(solution)/shard_map/ice_step/pallas_call | solution.py:780
  30.8 1.2 %hand_out.1 = (f32[2,256,256]{2,1,0:T(8,128)}, f32[8,5,32,256]{3,2,1,0:T(8,128)}) custom-call(f32[2,256,256]{2,1,0:T(8,128)S(1)} %get-tuple-element.4.flux, f32[8,5,32,256]{3,2,1,0:T(8,128)S(1)} %get-tuple-element.5.blocks), custom_call_target="tpu_custom_call" | custom-call | tf_op jit(solution)/shard_map/hand_out/pallas_call | solution.py:833
